TPU v7x, 32 devices: a whole 2x2x4 slice. The times are simulated.
32 devices in a mesh: parts: 2 (over y), clus: 16 (over z, x, core).
Axes of the slice: x: 2, y: 2, z: 4, core: 2. Of those that a mesh axis runs over, the one named last changes fastest.
Arguments:
- density: float32 [32, 512, 1024], P(('parts', 'clus')), parts along dimension 0, may hold values from -6 to 6
- positions: float32 [32, 3, 512], P(('parts', 'clus')), parts along dimension 0, may hold values from -0.36 to 1.36
- area: float32 [32, 512], P(('parts', 'clus')), parts along dimension 0, may hold values from 0.01 to 0.04
- incident: float32 [32, 512, 512], P(('parts', 'clus')), parts along dimension 0, may hold values from -6 to 6
- pair_list: int32 [64], P(('parts', 'clus')), parts along dimension 0, may hold values from 0 to 15, as said below
- pair_count: int32 [32], P(('parts', 'clus')), parts along dimension 0, may hold values from 1 to 2, as said below
Outputs:
- residual: float32 [32, 512, 512], P(('parts', 'clus')), parts along dimension 0
There are 2 independent parts, one for each index of `parts`. A program takes and returns all parts, laid end to end along the dimension named above; each array names one. Nothing has to cross between parts.
Inputs may be any that keep to these rules, and one draw needn't show every extreme that they name: `pair_list`: cluster k lies on device k of clus. Slots 2 q to 2 q + 1 belong to cluster q and name the clusters (q + d) mod 16 for distinct d in 1 .. 3; slots past pair_count[q] are ignored. `pair_count`: some cluster has exactly 2 live pairs.
All inputs are finite; a program needn't handle non-finite values.
Results may differ from a plain program's by a relative error of at most 0.0003.
Values sent between devices are 32-bit elements; how exact they have to be, the bound alone decides.
No kernel may reach another device: no remote copies, remote signals or barrier semaphores. Data moves between devices by JAX's collectives and lax.ppermute only.
A program may use at most 128 MiB of HBM per device.

v0:
```python
import math

import jax
import jax.numpy as jnp
import numpy as np
from jax import lax
from jax.experimental import pallas as pl
from jax.experimental.pallas import tpu as pltpu
from jax.sharding import PartitionSpec as P

COLS = 32
RADIUS = 0.95
SMOOTH = 0.01
TERMS = 23
SPAN = 4 * COLS
TILE_I = 256
TILE_J = 128
FLAG_ROW = 3
META = 8
F32 = jnp.float32
BF16 = jnp.bfloat16
VMEM_LIMIT = 60 * 1024 * 1024


def residue_map():
    eye = np.eye(16)
    plus, minus = eye[:8] + eye[8:], eye[:8] - eye[8:]
    rows = [plus[m] + plus[m + 4] for m in range(4)]
    rows += [plus[m] - plus[m + 4] for m in range(4)]
    w = np.exp(0.25j * np.pi)
    e = minus[:4] + 1j * minus[4:]
    for sign in (1.0, -1.0):
        pair = [e[m] + sign * w * e[m + 2] for m in range(2)]
        rows += [pair[0].real, pair[1].real, pair[0].imag, pair[1].imag]
    return np.stack(rows)


def fold_table():
    steps = np.arange(16)
    angles = 2.0 * np.pi * (np.outer(steps, steps) % 16) / 16
    fold = np.stack([np.cos(angles), -np.sin(angles)], axis=2).reshape(16, 32) / 16
    table = np.kron(residue_map() @ fold, np.eye(COLS)).astype(np.float32)
    high = table.astype(jnp.bfloat16)
    low = (table - high.astype(np.float32)).astype(jnp.bfloat16)
    return high, low


def scales():
    inv = [1.0] * (TERMS + 1)
    for n in range(3, TERMS):
        inv[n + 1] = inv[n] * 2.0 * RADIUS / (n + 1)
    return inv


def split(value):
    high = value.astype(BF16)
    return high, (value - high.astype(F32)).astype(BF16)


def dot_nt(left, right):
    return lax.dot_general(left, right, (((1,), (1,)), ((), ())), preferred_element_type=F32)


def live_ahead(listed, count, delta):
    devices = lax.axis_size("clus")
    wanted = lax.rem(lax.axis_index("clus") + delta + devices, devices)
    first = (listed[0] == wanted) & (count[0] > 0)
    second = (listed[1] == wanted) & (count[0] > 1)
    return first | second


def fold_kernel(density, area, place, listed, count, high, low, out, own):
    part_high, part_low = split(density[0])
    folded = dot_nt(high[...], part_high) + dot_nt(high[...], part_low) + dot_nt(low[...], part_high)
    rows = folded.shape[0]
    out[0:rows, :] = folded * area[...]
    for axis in range(3):
        out[rows + axis : rows + axis + 1, :] = place[axis]
    for ahead in range(1, 4):
        flag = jnp.where(live_ahead(listed, count, ahead), 1.0, 0.0).astype(F32)
        row = rows + FLAG_ROW + ahead - 1
        out[row : row + 1, :] = jnp.full((1, out.shape[1]), flag, F32)
    out[rows + 6 : rows + 8, :] = jnp.zeros((2, out.shape[1]), F32)
    panels = out.shape[1]
    for axis in range(3):
        spread = jnp.broadcast_to(place[axis], (128, panels))
        own[axis] = spread.T


def kernels(targets, sources):
    inv = scales()
    gaps = [a - b for a, b in zip(targets, sources)]
    square = gaps[0] * gaps[0] + gaps[1] * gaps[1] + gaps[2] * gaps[2] + SMOOTH
    inverse = lax.rsqrt(square)
    dist = square * inverse
    t = [jnp.exp(-1.5 * dist) * inverse]
    t.append((2.0 * RADIUS) * dist * t[0])
    for n in range(1, 3):
        t.append(dist * ((2.0 * RADIUS / (n + 1)) * t[n] - (RADIUS * RADIUS / (n + 1)) * t[n - 1]))
    for n in range(3, TERMS):
        factor = RADIUS * inv[n - 1] / (2.0 * inv[n])
        t.append(dist * (t[n] - factor * t[n - 1]))
    plus, minus = [], []
    for m in range(8):
        base = t[m]
        if m + 16 <= TERMS:
            base = base + (inv[m + 16] / inv[m]) * t[m + 16]
        other = (inv[m + 8] / inv[m]) * t[m + 8]
        plus.append(base + other)
        minus.append(base - other)
    first, second = [], []
    for m in range(4):
        other = inv[m + 4] * plus[m + 4]
        first.append(plus[m] + other)
        second.append(plus[m] - other)
    third, fourth = [], []
    half = math.sqrt(0.5)
    for m in range(2):
        a = half * minus[m + 2]
        b = (half * inv[m + 6]) * minus[m + 6]
        imag = inv[m + 4] * minus[m + 4]
        third += [minus[m] + (a - b), imag + (a + b)]
        fourth += [minus[m] - (a - b), imag - (a + b)]
    return first + second + third + fourth


def prepare(slot, payload, lhs, spots):
    panels = payload.shape[1]
    half = math.sqrt(0.5)
    rows = 16 * COLS
    for j in range(panels // TILE_J):
        at = slice(j * TILE_J, (j + 1) * TILE_J)
        spots[slot, j] = payload[rows : rows + META, at]

        def block(index):
            return payload[index * COLS : (index + 1) * COLS, at]

        def put(group, kernel, position, pieces):
            lanes = slice(kernel * TILE_J, (kernel + 1) * TILE_J)
            top = position * COLS
            lhs[slot, group, j, top : top + COLS, lanes] = pieces[0]
            lhs[slot, group, j, SPAN + top : SPAN + top + COLS, lanes] = pieces[1]

        def minus(pieces):
            return (-pieces[0], -pieces[1])

        for group in range(2):
            pieces = [split(block(group * 4 + n)) for n in range(4)]
            flipped = [minus(p) for p in pieces] if group else pieces
            for k in range(4):
                for n in range(4):
                    put(group, k, n, pieces[n - k] if n >= k else flipped[n - k + 4])
        for group in range(2, 4):
            raw = [block(group * 4 + n) for n in range(4)]
            x0r, x1r, x0i, x1i = [split(r) for r in raw]
            sign = half if group == 2 else -half
            wr = split(sign * (raw[1] - raw[3]))
            wi = split(sign * (raw[1] + raw[3]))
            table = (
                (x0r, x1r, x0i, x1i),
                (minus(x0i), minus(x1i), x0r, x1r),
                (wr, x0r, wi, x0i),
                (minus(wi), minus(x0i), wr, x0r),
            )
            for k in range(4):
                for n in range(4):
                    put(group, k, n, table[k][n])


def near_kernel(offsets, has_input, *refs):
    count = len(offsets)
    listed, live_count, own = refs[:3]
    payloads = refs[3 : 3 + count]
    rest = refs[3 + count :]
    turn = 1 - 2 * lax.rem(lax.axis_index("clus"), 2)
    if has_input:
        rest = rest[1:]
    out, acc, lhs, spots, high0, low0, high1, low1 = rest
    acc[:, SPAN : 2 * SPAN, :] = jnp.zeros((4, SPAN, acc.shape[2]), F32)
    acc[:, 0:SPAN, :] = refs[3 + count][...] if has_input else jnp.zeros((4, SPAN, acc.shape[2]), F32)
    high1[...] = jnp.zeros_like(high1)
    low1[...] = jnp.zeros_like(low1)
    rows = 16 * COLS
    total = jnp.int32(0)
    for s in range(count):
        delta = offsets[s][0] + offsets[s][1] * turn
        ahead = live_ahead(listed, live_count, delta)
        row = rows + FLAG_ROW - 1 + jnp.clip(-delta, 1, 3)
        flag = jnp.max(payloads[s][pl.ds(row, 1), :])
        live = (delta == 0) | ((delta > 0) & ahead) | ((delta < 0) & (flag > 0.5))

        @pl.when(live)
        def _():
            prepare(total, payloads[s], lhs, spots)

        total = total + live.astype(jnp.int32)

    def evaluate(slot, j, i, high, low, quarter):
        step = TILE_I // 4
        spot = spots[slot, j]
        sources = [jnp.broadcast_to(spot[a : a + 1, :], (16, TILE_J)) for a in range(3)]
        for r in range(quarter * step, (quarter + 1) * step, 16):
            targets = [own[a, i * TILE_I + r : i * TILE_I + r + 16, :] for a in range(3)]
            for index, value in enumerate(kernels(targets, sources)):
                top, bottom = split(value)
                lanes = slice((index % 4) * TILE_J, (index % 4 + 1) * TILE_J)
                high[index // 4, r : r + 16, lanes] = top
                low[index // 4, r : r + 16, lanes] = bottom

    def apply(slot, j, i, high, low, group):
        left = lhs[slot, group, j]
        at = slice(i * TILE_I, (i + 1) * TILE_I)
        acc[group, :, at] += dot_nt(left, high[group])
        acc[group, 0:SPAN, at] += dot_nt(left[0:SPAN], low[group])

    tiles = own.shape[1] // TILE_J

    def step(index, carry):
        slot, j = index // tiles, index % tiles
        before = jnp.maximum(index - 1, 0)
        slot_before, j_before = before // tiles, before % tiles
        for quarter in range(4):
            evaluate(slot, j, 0, high0, low0, quarter)
            apply(slot_before, j_before, 1, high1, low1, quarter)
        for quarter in range(4):
            evaluate(slot, j, 1, high1, low1, quarter)
            apply(slot, j, 0, high0, low0, quarter)
        return carry

    lax.fori_loop(0, total * tiles, step, 0)

    @pl.when(total > 0)
    def _():
        for group in range(4):
            apply(total - 1, tiles - 1, 1, high1, low1, group)

    out[...] = acc[:, 0:SPAN, :] + acc[:, SPAN : 2 * SPAN, :]


def near_call(pairs, own, offsets, payloads, acc):
    count = len(payloads)
    panels = own.shape[1]
    tiles = panels // TILE_J
    shape = jax.ShapeDtypeStruct((4, SPAN, panels), F32)
    vmem = pl.BlockSpec(memory_space=pltpu.VMEM)
    smem = pl.BlockSpec(memory_space=pltpu.SMEM)
    arguments = [*pairs, own, *payloads] + ([] if acc is None else [acc])
    return pl.pallas_call(
        lambda *refs: near_kernel(offsets, acc is not None, *refs),
        out_shape=shape,
        in_specs=[smem] * 2 + [vmem] * (len(arguments) - 2),
        out_specs=vmem,
        scratch_shapes=[
            pltpu.VMEM((4, 2 * SPAN, panels), F32),
            pltpu.VMEM((count, 4, tiles, 2 * SPAN, 4 * TILE_J), BF16),
            pltpu.VMEM((count, tiles, META, TILE_J), F32),
        ]
        + [pltpu.VMEM((4, TILE_I, 4 * TILE_J), BF16)] * 4,
        compiler_params=pltpu.CompilerParams(vmem_limit_bytes=VMEM_LIMIT),
        cost_estimate=pl.CostEstimate(
            flops=count * 2 * 32768 * 256 * 256 // 2, bytes_accessed=4 << 20, transcendentals=0
        ),
        name="near",
    )(*arguments)


def final_kernel(acc, incident, out):
    panels = acc.shape[2]
    half = math.sqrt(0.5)
    for lane in range(0, panels, 128):
        at = slice(lane, lane + 128)
        parts = []
        for group in range(4):
            whole = acc[group, :, at]
            parts.append([whole[n * COLS : (n + 1) * COLS] for n in range(4)])
        first, second, third, fourth = parts
        plus = [first[n] + second[n] for n in range(4)] + [first[n] - second[n] for n in range(4)]
        minus = [None] * 8
        for m in range(2):
            sum_r, sum_i = third[m] + fourth[m], third[m + 2] + fourth[m + 2]
            gap_r, gap_i = third[m] - fourth[m], third[m + 2] - fourth[m + 2]
            minus[m], minus[m + 4] = sum_r, sum_i
            minus[m + 2] = half * (gap_r + gap_i)
            minus[m + 6] = half * (gap_i - gap_r)
        steps = [None] * 16
        for m in range(8):
            low = plus[m] + minus[m]
            high = plus[m] - minus[m]
            for n, value in ((-m % 16, low), ((-m - 8) % 16, high)):
                steps[n] = value * (0.25 * RADIUS ** (-n))
        potential = jnp.concatenate(steps, axis=0).T
        out[0, at, :] = incident[0, at, :] - potential


def residual(density, positions, area, incident, pair_list, pair_count):
    devices = lax.axis_size("clus")
    panels = positions.shape[2]
    pairs = (pair_list, pair_count)
    table_high, table_low = fold_table()
    vmem = pl.BlockSpec(memory_space=pltpu.VMEM)
    smem = pl.BlockSpec(memory_space=pltpu.SMEM)
    payload, own = pl.pallas_call(
        fold_kernel,
        out_shape=(
            jax.ShapeDtypeStruct((16 * COLS + META, panels), F32),
            jax.ShapeDtypeStruct((3, panels, 128), F32),
        ),
        in_specs=[vmem, vmem, vmem, smem, smem, vmem, vmem],
        out_specs=(vmem, vmem),
        compiler_params=pltpu.CompilerParams(vmem_limit_bytes=VMEM_LIMIT),
        name="fold",
    )(density, area, positions.transpose(1, 0, 2), *pairs, jnp.asarray(table_high), jnp.asarray(table_low))

    def route(value, move, members=lambda k: True):
        pairs_of = [(k, move(k) % devices) for k in range(devices) if members(k)]
        return lax.ppermute(value, "clus", pairs_of)

    def swap(value):
        return route(value, lambda k: k ^ 1)

    partner = swap(payload)
    ahead = route(payload, lambda k: k - 2)
    far = route(payload, lambda k: k - 3 if k % 2 == 0 else k + 3)
    behind = route(payload, lambda k: k + 2)
    acc = near_call(pairs, own, ((0, 0), (0, 1)), (payload, partner), None)
    ahead_other = swap(ahead)
    acc = near_call(pairs, own, ((2, 0),), (ahead,), acc)
    acc = near_call(pairs, own, ((2, 1), (0, -3)), (ahead_other, far), acc)
    behind_other = swap(behind)
    acc = near_call(pairs, own, ((-2, 0),), (behind,), acc)
    acc = near_call(pairs, own, ((-2, 1),), (behind_other,), acc)
    return pl.pallas_call(
        final_kernel,
        out_shape=jax.ShapeDtypeStruct(incident.shape, F32),
        in_specs=[vmem, vmem],
        out_specs=vmem,
        compiler_params=pltpu.CompilerParams(vmem_limit_bytes=VMEM_LIMIT),
        name="final",
    )(acc, incident)


def solution(mesh):
    spec3 = P(("parts", "clus"), None, None)
    in_specs = (spec3, spec3, P(("parts", "clus"), None), spec3, P(("parts", "clus")), P(("parts", "clus")))
    return jax.shard_map(residual, mesh=mesh, in_specs=in_specs, out_specs=spec3, check_vma=False)
```

profile of v0, /device:TPU:1, one launch (start us, length us, event | category | flops | bytes accessed | tf_op | source)
XLA Modules:
  0.0 152.0 jit_solution(17224403555926669675)
XLA Ops:
  0.7 5.2 %fold.1 = (f32[520,512]{1,0:T(8,128)}, f32[3,512,128]{2,1,0:T(8,128)}) custom-call(f32[1,512,1024]{2,1,0:T(8,128)} %density.1, f32[1,512]{1,0:T(1,128)} %area.1, f32[3,1,512]{2,1,0:T(1,128)} %bitcast.1, s32[2]{0:T(128)} %refs_0_.9, s32[1]{0:T(128)S(6)} %copy.9.count.refs_1_, bf16[512,1024]{1,0:T(8,128)(2,1)} %constant.4.clone.high, ...), custom_call_target="tpu_custom_call" | custom-call | tf_op jit(solution)/shard_map/fold/pallas_call | solution.py:302
  5.9 5.1 %collective-permute-start.2 = (f32[520,512]{1,0:T(8,128)}, f32[520,512]{1,0:T(8,128)S(1)}, u32[]{:S(2)}, u32[]{:S(2)}) collective-permute-start(f32[520,512]{1,0:T(8,128)} %get-tuple-element.8.refs_3_), channel_id=1, source_target_pairs={{0,14},{1,15},{2,0},{3,1},{4,2},{5,3},{6,4},{7,5},{8,6},{9,7},{10,... | collective-permute-start | bytes 3194888 | tf_op jit(solution)/shard_map/ppermute | solution.py:316
  10.9 0.0 collective-permute-start
  10.9 1.0 collective-permute-start.5
  11.9 0.0 collective-permute-start.4
  11.9 42.2 %collective-permute-done.2.refs_3_ = f32[520,512]{1,0:T(8,128)S(1)} collective-permute-done((f32[520,512]{1,0:T(8,128)}, f32[520,512]{1,0:T(8,128)S(1)}, u32[]{:S(2)}, u32[]{:S(2)}) %collective-permute-start.2) | collective-permute-done | bytes 1064992 | tf_op jit(solution)/shard_map/ppermute | solution.py:316
  54.1 0.0 copy-start.1
  54.2 1.3 collective-permute-start.3
  55.4 0.0 collective-permute-done.refs_3_
  55.4 0.0 copy-start
  55.4 0.3 collective-permute-start.1
  55.7 0.0 collective-permute-done.5.refs_4_
  55.7 28.0 %near.5.refs_4_ = f32[4,128,512]{2,1,0:T(8,128)} custom-call(s32[2]{0:T(128)} %refs_0_.9, s32[1]{0:T(128)S(6)} %copy.9.count.refs_1_, f32[3,512,128]{2,1,0:T(8,128)} %get-tuple-element.7.refs_2_, f32[520,512]{1,0:T(8,128)} %get-tuple-element.8.refs_3_, f32[520,512]{1,0:T(8,128)} %collective-permute-done.5.refs_4_), custom_call_target="tpu_custom_call" | custom-call | flops 4294967296 | bytes 4194304 | tf_op jit(solution)/shard_map/near/pallas_call | solution.py:248
  83.7 0.0 copy-done.1
  83.7 0.0 copy-done
  83.7 15.9 %near.6.refs_5_ = f32[4,128,512]{2,1,0:T(8,128)} custom-call(s32[2]{0:T(128)} %refs_0_.9, s32[1]{0:T(128)S(6)} %copy.9.count.refs_1_, f32[3,512,128]{2,1,0:T(8,128)} %get-tuple-element.7.refs_2_, f32[520,512]{1,0:T(8,128)} %copy-done.1, f32[4,128,512]{2,1,0:T(8,128)} %near.5.refs_4_), custom_call_target="tpu_custom_call" | custom-call | flops 2147483648 | bytes 4194304 | tf_op jit(solution)/shard_map/near/pallas_call | solution.py:248
  99.6 0.0 collective-permute-done.4.refs_4_
  99.6 0.0 copy-start.2
  99.6 0.0 collective-permute-done.3.refs_3_
  99.6 1.0 copy-done.2
  100.6 16.6 %near.7.refs_4_ = f32[4,128,512]{2,1,0:T(8,128)} custom-call(s32[2]{0:T(128)} %refs_0_.9, s32[1]{0:T(128)S(6)} %copy.9.count.refs_1_, f32[3,512,128]{2,1,0:T(8,128)} %get-tuple-element.7.refs_2_, f32[520,512]{1,0:T(8,128)} %collective-permute-done.3.refs_3_, f32[520,512]{1,0:T(8,128)} %copy-done.2, f32[4,128,512]{2,1,0:T(8,128)} %near.6.refs_5_), custom_call_target="tpu_custom_call" | custom-call | flops 4294967296 | bytes 4194304 | tf_op jit(solution)/shard_map/near/pallas_call | solution.py:248
  117.1 16.0 %near.8.refs_4_ = f32[4,128,512]{2,1,0:T(8,128)} custom-call(s32[2]{0:T(128)} %refs_0_.9, s32[1]{0:T(128)S(6)} %copy.9.count.refs_1_, f32[3,512,128]{2,1,0:T(8,128)} %get-tuple-element.7.refs_2_, f32[520,512]{1,0:T(8,128)} %copy-done, f32[4,128,512]{2,1,0:T(8,128)} %near.7.refs_4_), custom_call_target="tpu_custom_call" | custom-call | flops 2147483648 | bytes 4194304 | tf_op jit(solution)/shard_map/near/pallas_call | solution.py:248
  133.1 0.0 collective-permute-done.1.refs_3_
  133.1 16.0 %near.9.acc = f32[4,128,512]{2,1,0:T(8,128)} custom-call(s32[2]{0:T(128)} %refs_0_.9, s32[1]{0:T(128)S(6)} %copy.9.count.refs_1_, f32[3,512,128]{2,1,0:T(8,128)} %get-tuple-element.7.refs_2_, f32[520,512]{1,0:T(8,128)} %collective-permute-done.1.refs_3_, f32[4,128,512]{2,1,0:T(8,128)} %near.8.refs_4_), custom_call_target="tpu_custom_call" | custom-call | flops 2147483648 | bytes 4194304 | tf_op jit(solution)/shard_map/near/pallas_call | solution.py:248
  149.1 2.9 %final.1 = f32[1,512,512]{2,1,0:T(8,128)} custom-call(f32[4,128,512]{2,1,0:T(8,128)} %near.9.acc, f32[1,512,512]{2,1,0:T(8,128)} %incident.1), custom_call_target="tpu_custom_call" | custom-call | tf_op jit(solution)/shard_map/final/pallas_call | solution.py:332
Async XLA Ops:
  5.9 48.3 %collective-permute-start.2 = (f32[520,512]{1,0:T(8,128)}, f32[520,512]{1,0:T(8,128)S(1)}, u32[]{:S(2)}, u32[]{:S(2)}) collective-permute-start(f32[520,512]{1,0:T(8,128)} %get-tuple-element.8.refs_3_), channel_id=1, source_target_pairs={{0,14},{1,15},{2,0},{3,1},{4,2},{5,3},{6,4},{7,5},{8,6},{9,7},{10,... | collective-permute-start | bytes 3194888 | tf_op jit(solution)/shard_map/ppermute | solution.py:316
  10.9 44.5 %collective-permute-start = (f32[520,512]{1,0:T(8,128)}, f32[520,512]{1,0:T(8,128)S(1)}, u32[]{:S(2)}, u32[]{:S(2)}) collective-permute-start(f32[520,512]{1,0:T(8,128)} %get-tuple-element.8.refs_3_), channel_id=1, source_target_pairs={{0,2},{1,3},{2,4},{3,5},{4,6},{5,7},{6,8},{7,9},{8,10},{9,11},{10,... | collective-permute-start | bytes 3194888 | tf_op jit(solution)/shard_map/ppermute | solution.py:316
  10.9 44.7 %collective-permute-start.5 = (f32[520,512]{1,0:T(8,128)}, f32[520,512]{1,0:T(8,128)}, u32[]{:S(2)}, u32[]{:S(2)}) collective-permute-start(f32[520,512]{1,0:T(8,128)} %get-tuple-element.8.refs_3_), channel_id=1, source_target_pairs={{0,1},{1,0},{2,3},{3,2},{4,5},{5,4},{6,7},{7,6},{8,9},{9,8},{10,11... | collective-permute-start | bytes 3194888 | tf_op jit(solution)/shard_map/ppermute | solution.py:316
  11.9 87.7 %collective-permute-start.4 = (f32[520,512]{1,0:T(8,128)}, f32[520,512]{1,0:T(8,128)S(1)}, u32[]{:S(2)}, u32[]{:S(2)}) collective-permute-start(f32[520,512]{1,0:T(8,128)} %get-tuple-element.8.refs_3_), channel_id=1, source_target_pairs={{0,13},{1,4},{2,15},{3,6},{4,1},{5,8},{6,3},{7,10},{8,5},{9,12},{1... | collective-permute-start | bytes 3194888 | tf_op jit(solution)/shard_map/ppermute | solution.py:316
  54.1 29.5 %copy-start.1 = (f32[520,512]{1,0:T(8,128)}, f32[520,512]{1,0:T(8,128)S(1)}, u32[]{:S(2)}) copy-start(f32[520,512]{1,0:T(8,128)S(1)} %collective-permute-done.2.refs_3_) | copy-start | bytes 3194884
  54.2 45.4 %collective-permute-start.3 = (f32[520,512]{1,0:T(8,128)S(1)}, f32[520,512]{1,0:T(8,128)}, u32[]{:S(2)}, u32[]{:S(2)}) collective-permute-start(f32[520,512]{1,0:T(8,128)S(1)} %collective-permute-done.2.refs_3_), channel_id=1, source_target_pairs={{0,1},{1,0},{2,3},{3,2},{4,5},{5,4},{6,7},{7,6},{8,9},{9,8},{10,11... | collective-permute-start | bytes 3194888 | tf_op jit(solution)/shard_map/ppermute | solution.py:316
  55.4 28.3 %copy-start = (f32[520,512]{1,0:T(8,128)}, f32[520,512]{1,0:T(8,128)S(1)}, u32[]{:S(2)}) copy-start(f32[520,512]{1,0:T(8,128)S(1)} %collective-permute-done.refs_3_) | copy-start | bytes 3194884
  55.4 77.7 %collective-permute-start.1 = (f32[520,512]{1,0:T(8,128)S(1)}, f32[520,512]{1,0:T(8,128)}, u32[]{:S(2)}, u32[]{:S(2)}) collective-permute-start(f32[520,512]{1,0:T(8,128)S(1)} %collective-permute-done.refs_3_), channel_id=1, source_target_pairs={{0,1},{1,0},{2,3},{3,2},{4,5},{5,4},{6,7},{7,6},{8,9},{9,8},{10,11... | collective-permute-start | bytes 3194888 | tf_op jit(solution)/shard_map/ppermute | solution.py:316
  99.6 1.0 copy-start.2
where the time goes:
time: 152 us
  Pallas kernels  101 us (66%)
  waiting for transfers between devices  42.3 us (28%)
  starting transfers between devices  7.55 us (5%)
    pallas_call x5, Pallas kernels, near_call(): pl.pallas_call(lambda *refs: near_kernel(offsets, acc is not None, *refs)...  92.5 us
    ppermute x6, waiting for transfers between devices, route(): return lax.ppermute(value, 'clus', pairs_of)  42.3 us
    ppermute x6, starting transfers between devices, route(): return lax.ppermute(value, 'clus', pairs_of)  7.55 us
    pallas_call x1, Pallas kernels, residual(): pl.pallas_call(fold_kernel, out_shape=(jax.ShapeDtypeStruct((16 * COLS +...  5.21 us
  transfers between devices with their start and end apart: 6, of which 1 were waited for; matrix products, arithmetic and copies ran while one was open for 0% of the time, Pallas kernels for 50%

commit v1 on v0

--- a/solution.py
+++ b/solution.py
@@ -14,12 +14,15 @@
 TERMS = 23
 SPAN = 4 * COLS
 TILE_I = 256
-TILE_J = 128
+TILE_J = 256
+LANES = 128
+KPART = 4
 FLAG_ROW = 3
 META = 8
 F32 = jnp.float32
 BF16 = jnp.bfloat16
 VMEM_LIMIT = 60 * 1024 * 1024
+NEAR_LIMIT = 67043328
 
 
 def residue_map():
@@ -128,90 +131,134 @@
     panels = payload.shape[1]
     half = math.sqrt(0.5)
     rows = 16 * COLS
-    for j in range(panels // TILE_J):
-        at = slice(j * TILE_J, (j + 1) * TILE_J)
+
+    def column(j, carry):
+        at = pl.ds(pl.multiple_of(j * LANES, LANES), LANES)
         spots[slot, j] = payload[rows : rows + META, at]
 
-        def block(index):
-            return payload[index * COLS : (index + 1) * COLS, at]
-
-        def put(group, kernel, position, pieces):
-            lanes = slice(kernel * TILE_J, (kernel + 1) * TILE_J)
-            top = position * COLS
-            lhs[slot, group, j, top : top + COLS, lanes] = pieces[0]
-            lhs[slot, group, j, SPAN + top : SPAN + top + COLS, lanes] = pieces[1]
-
-        def minus(pieces):
-            return (-pieces[0], -pieces[1])
-
-        for group in range(2):
-            pieces = [split(block(group * 4 + n)) for n in range(4)]
-            flipped = [minus(p) for p in pieces] if group else pieces
-            for k in range(4):
-                for n in range(4):
-                    put(group, k, n, pieces[n - k] if n >= k else flipped[n - k + 4])
-        for group in range(2, 4):
-            raw = [block(group * 4 + n) for n in range(4)]
-            x0r, x1r, x0i, x1i = [split(r) for r in raw]
-            sign = half if group == 2 else -half
-            wr = split(sign * (raw[1] - raw[3]))
-            wi = split(sign * (raw[1] + raw[3]))
-            table = (
-                (x0r, x1r, x0i, x1i),
-                (minus(x0i), minus(x1i), x0r, x1r),
-                (wr, x0r, wi, x0i),
-                (minus(wi), minus(x0i), wr, x0r),
-            )
-            for k in range(4):
-                for n in range(4):
-                    put(group, k, n, table[k][n])
+        def block(index, part):
+            top = index * COLS + part * 16
+            return payload[top : top + 16, at]
+
+        def put(kernel, position, part, pieces):
+            top = position * COLS + part * 16
+            lhs[slot, kernel, j, top : top + 16, :] = pieces[0]
+            lhs[slot, kernel, j, SPAN + top : SPAN + top + 16, :] = pieces[1]
+
+        for group in range(4):
+            for part in range(COLS // 16):
+                raw = [block(group * 4 + n, part) for n in range(4)]
+                if group < 2:
+                    pieces = [split(r) for r in raw]
+                    flipped = [split(-r) for r in raw] if group else pieces
+                    table = [
+                        [pieces[n - k] if n >= k else flipped[n - k + 4] for n in range(4)]
+                        for k in range(4)
+                    ]
+                else:
+                    sign = half if group == 2 else -half
+                    x0r, x1r, x0i, x1i = [split(r) for r in raw]
+                    n0i, n1i = split(-raw[2]), split(-raw[3])
+                    turned = sign * (raw[1] + raw[3])
+                    wr, wi, nwi = split(sign * (raw[1] - raw[3])), split(turned), split(-turned)
+                    table = [
+                        [x0r, x1r, x0i, x1i],
+                        [n0i, n1i, x0r, x1r],
+                        [wr, x0r, wi, x0i],
+                        [nwi, n0i, wr, x0r],
+                    ]
+                for k in range(4):
+                    for n in range(4):
+                        put(group * 4 + k, n, part, table[k][n])
+        return carry
+
+    lax.fori_loop(0, panels // LANES, column, 0)
 
 
 def near_kernel(offsets, has_input, *refs):
     count = len(offsets)
-    listed, live_count, own = refs[:3]
-    payloads = refs[3 : 3 + count]
+    listed, live_count, own_hbm = refs[:3]
+    payload_hbm = refs[3 : 3 + count]
     rest = refs[3 + count :]
+    before_hbm = rest[0] if has_input else None
+    out_hbm, payloads, own, acc, lhs, spots, high0, low0, high1, low1, sems = rest[-11:]
     turn = 1 - 2 * lax.rem(lax.axis_index("clus"), 2)
-    if has_input:
-        rest = rest[1:]
-    out, acc, lhs, spots, high0, low0, high1, low1 = rest
-    acc[:, SPAN : 2 * SPAN, :] = jnp.zeros((4, SPAN, acc.shape[2]), F32)
-    acc[:, 0:SPAN, :] = refs[3 + count][...] if has_input else jnp.zeros((4, SPAN, acc.shape[2]), F32)
-    high1[...] = jnp.zeros_like(high1)
-    low1[...] = jnp.zeros_like(low1)
+    loads = [
+        pltpu.make_async_copy(payload_hbm[s], payloads.at[s], sems.at[2 + s]) for s in range(count)
+    ]
+    for load in loads:
+        load.start()
+    own_load = pltpu.make_async_copy(own_hbm, own, sems.at[0])
+    head = acc.at[:, 0:SPAN, :]
     rows = 16 * COLS
-    total = jnp.int32(0)
+    lives = []
     for s in range(count):
+        loads[s].wait()
         delta = offsets[s][0] + offsets[s][1] * turn
         ahead = live_ahead(listed, live_count, delta)
         row = rows + FLAG_ROW - 1 + jnp.clip(-delta, 1, 3)
-        flag = jnp.max(payloads[s][pl.ds(row, 1), :])
+        flag = jnp.max(payloads[s, pl.ds(row, 1), :])
         live = (delta == 0) | ((delta > 0) & ahead) | ((delta < 0) & (flag > 0.5))
-
-        @pl.when(live)
+        lives.append(live.astype(jnp.int32))
+    total = sum(lives[1:], lives[0])
+
+    @pl.when(total > 0)
+    def _():
+        near_body(has_input, lives, total, own_load, before_hbm, payloads, own, acc, head, lhs, spots,
+                  high0, low0, high1, low1, sems)
+        store = pltpu.make_async_copy(head, out_hbm, sems.at[1])
+        store.start()
+        store.wait()
+
+
+def near_body(has_input, lives, total, own_load, before_hbm, payloads, own, acc, head, lhs, spots,
+              high0, low0, high1, low1, sems):
+    own_load.start()
+    if has_input:
+        before_load = pltpu.make_async_copy(before_hbm, head, sems.at[1])
+        before_load.start()
+    else:
+        head[...] = jnp.zeros(head.shape, F32)
+    acc[:, SPAN : 2 * SPAN, :] = jnp.zeros(head.shape, F32)
+    high1[...] = jnp.zeros_like(high1)
+    low1[...] = jnp.zeros_like(low1)
+    slot_of = jnp.int32(0)
+    for s, live in enumerate(lives):
+
+        @pl.when(live > 0)
         def _():
-            prepare(total, payloads[s], lhs, spots)
-
-        total = total + live.astype(jnp.int32)
+            prepare(slot_of, payloads.at[s], lhs, spots)
+
+        slot_of = slot_of + live
+    own_load.wait()
+    if has_input:
+        before_load.wait()
+    halves = TILE_J // LANES
 
     def evaluate(slot, j, i, high, low, quarter):
-        step = TILE_I // 4
-        spot = spots[slot, j]
-        sources = [jnp.broadcast_to(spot[a : a + 1, :], (16, TILE_J)) for a in range(3)]
-        for r in range(quarter * step, (quarter + 1) * step, 16):
-            targets = [own[a, i * TILE_I + r : i * TILE_I + r + 16, :] for a in range(3)]
-            for index, value in enumerate(kernels(targets, sources)):
-                top, bottom = split(value)
-                lanes = slice((index % 4) * TILE_J, (index % 4 + 1) * TILE_J)
-                high[index // 4, r : r + 16, lanes] = top
-                low[index // 4, r : r + 16, lanes] = bottom
-
-    def apply(slot, j, i, high, low, group):
-        left = lhs[slot, group, j]
+        steps = KPART
+        for r in range(steps):
+            row = pl.multiple_of((quarter * steps + r) * 16, 16)
+            targets = [own[a, pl.ds(i * TILE_I + row, 16), :] for a in range(3)]
+            for h in range(halves):
+                spot = spots[slot, j * halves + h]
+                sources = [jnp.broadcast_to(spot[a : a + 1, :], (16, LANES)) for a in range(3)]
+                values = kernels(targets, sources)
+                for index, value in enumerate(values):
+                    top, bottom = split(value)
+                    high[index, h, pl.ds(row, 16), :] = top
+                    low[index, h, pl.ds(row, 16), :] = bottom
+
+    def joined(read):
+        return jnp.concatenate([read(k, h) for k in range(KPART) for h in range(halves)], axis=1)
+
+    def apply(slot, j, i, high, low, part):
+        first = part * KPART
+        group = first // 4
+        left = joined(lambda k, h: lhs[slot, first + k, j * halves + h])
         at = slice(i * TILE_I, (i + 1) * TILE_I)
-        acc[group, :, at] += dot_nt(left, high[group])
-        acc[group, 0:SPAN, at] += dot_nt(left[0:SPAN], low[group])
+        acc[group, :, at] += dot_nt(left, joined(lambda k, h: high[first + k, h]))
+        acc[group, 0:SPAN, at] += dot_nt(left[0:SPAN], joined(lambda k, h: low[first + k, h]))
 
     tiles = own.shape[1] // TILE_J
 
@@ -219,46 +266,57 @@
         slot, j = index // tiles, index % tiles
         before = jnp.maximum(index - 1, 0)
         slot_before, j_before = before // tiles, before % tiles
-        for quarter in range(4):
-            evaluate(slot, j, 0, high0, low0, quarter)
-            apply(slot_before, j_before, 1, high1, low1, quarter)
-        for quarter in range(4):
-            evaluate(slot, j, 1, high1, low1, quarter)
-            apply(slot, j, 0, high0, low0, quarter)
+
+        def first(r, c):
+            evaluate(slot, j, 0, high0, low0, r)
+            apply(slot_before, j_before, 1, high1, low1, r)
+            return c
+
+        def second(r, c):
+            evaluate(slot, j, 1, high1, low1, r)
+            apply(slot, j, 0, high0, low0, r)
+            return c
+
+        lax.fori_loop(0, 16 // KPART, first, 0)
+        lax.fori_loop(0, 16 // KPART, second, 0)
         return carry
 
     lax.fori_loop(0, total * tiles, step, 0)
 
-    @pl.when(total > 0)
-    def _():
-        for group in range(4):
-            apply(total - 1, tiles - 1, 1, high1, low1, group)
-
-    out[...] = acc[:, 0:SPAN, :] + acc[:, SPAN : 2 * SPAN, :]
+    def last(part, c):
+        apply(total - 1, tiles - 1, 1, high1, low1, part)
+        return c
+
+    lax.fori_loop(0, 16 // KPART, last, 0)
+    head[...] = acc[:, 0:SPAN, :] + acc[:, SPAN : 2 * SPAN, :]
 
 
 def near_call(pairs, own, offsets, payloads, acc):
     count = len(payloads)
     panels = own.shape[1]
-    tiles = panels // TILE_J
+    tiles = panels // LANES
     shape = jax.ShapeDtypeStruct((4, SPAN, panels), F32)
-    vmem = pl.BlockSpec(memory_space=pltpu.VMEM)
+    anywhere = pl.BlockSpec(memory_space=pl.ANY)
     smem = pl.BlockSpec(memory_space=pltpu.SMEM)
     arguments = [*pairs, own, *payloads] + ([] if acc is None else [acc])
     return pl.pallas_call(
         lambda *refs: near_kernel(offsets, acc is not None, *refs),
         out_shape=shape,
-        in_specs=[smem] * 2 + [vmem] * (len(arguments) - 2),
-        out_specs=vmem,
+        in_specs=[smem] * 2 + [anywhere] * (len(arguments) - 2),
+        out_specs=anywhere,
+        input_output_aliases={} if acc is None else {len(arguments) - 1: 0},
         scratch_shapes=[
+            pltpu.VMEM((count,) + payloads[0].shape, F32),
+            pltpu.VMEM(own.shape, F32),
             pltpu.VMEM((4, 2 * SPAN, panels), F32),
-            pltpu.VMEM((count, 4, tiles, 2 * SPAN, 4 * TILE_J), BF16),
-            pltpu.VMEM((count, tiles, META, TILE_J), F32),
+            pltpu.VMEM((count, 16, tiles, 2 * SPAN, LANES), BF16),
+            pltpu.VMEM((count, tiles, META, LANES), F32),
         ]
-        + [pltpu.VMEM((4, TILE_I, 4 * TILE_J), BF16)] * 4,
-        compiler_params=pltpu.CompilerParams(vmem_limit_bytes=VMEM_LIMIT),
+        + [pltpu.VMEM((16, TILE_J // LANES, TILE_I, LANES), BF16)] * 4
+        + [pltpu.SemaphoreType.DMA((2 + count,))],
+        compiler_params=pltpu.CompilerParams(vmem_limit_bytes=NEAR_LIMIT),
         cost_estimate=pl.CostEstimate(
-            flops=count * 2 * 32768 * 256 * 256 // 2, bytes_accessed=4 << 20, transcendentals=0
+            flops=count * 2 * 32768 * 256 * 256, bytes_accessed=4 << 20, transcendentals=0
         ),
         name="near",
     )(*arguments)
@@ -324,11 +382,9 @@
     behind = route(payload, lambda k: k + 2)
     acc = near_call(pairs, own, ((0, 0), (0, 1)), (payload, partner), None)
     ahead_other = swap(ahead)
-    acc = near_call(pairs, own, ((2, 0),), (ahead,), acc)
-    acc = near_call(pairs, own, ((2, 1), (0, -3)), (ahead_other, far), acc)
+    acc = near_call(pairs, own, ((2, 0), (2, 1)), (ahead, ahead_other), acc)
     behind_other = swap(behind)
-    acc = near_call(pairs, own, ((-2, 0),), (behind,), acc)
-    acc = near_call(pairs, own, ((-2, 1),), (behind_other,), acc)
+    acc = near_call(pairs, own, ((-2, 0), (-2, 1), (0, -3)), (behind, behind_other, far), acc)
     return pl.pallas_call(
         final_kernel,
         out_shape=jax.ShapeDtypeStruct(incident.shape, F32),

time: 152 us -> 143 us (0.941)
  Pallas kernels: 101 us -> 88 us
  starting transfers between devices: 7.55 us -> 11.2 us
    pallas_call x5 -> x3, Pallas kernels: 92.5 us -> 79.9 us  [near_call(): pl.pallas_call(lambda *refs: near_kernel(offsets, acc is not None, *refs)...]
    ppermute x6, starting transfers between devices: 7.55 us -> 11.2 us  [route(): return lax.ppermute(value, 'clus', pairs_of)]
  transfers between devices with their start and end apart: 6 -> 6, of which waited for: 1 -> 1; matrix products, arithmetic and copies ran while one was open for 0% -> 0% of each run, Pallas kernels for 50% -> 37%
where the time goes in v1:
time: 143 us; the launch traced here: 142 us
  Pallas kernels  88 us (62%)
  waiting for transfers between devices  42.4 us (30%)
  starting transfers between devices  11.2 us (8%)
    pallas_call x3, Pallas kernels, near_call(): pl.pallas_call(lambda *refs: near_kernel(offsets, acc is not None, *refs)...  79.9 us
    ppermute x6, waiting for transfers between devices, route(): return lax.ppermute(value, 'clus', pairs_of)  42.4 us
    ppermute x6, starting transfers between devices, route(): return lax.ppermute(value, 'clus', pairs_of)  11.2 us
    pallas_call x1, Pallas kernels, residual(): pl.pallas_call(fold_kernel, out_shape=(jax.ShapeDtypeStruct((16 * COLS +...  5.23 us
    pallas_call x1, Pallas kernels, residual(): pl.pallas_call(final_kernel, out_shape=jax.ShapeDtypeStruct(incident.shap...  2.87 us
  transfers between devices with their start and end apart: 6, of which 1 were waited for; matrix products, arithmetic and copies ran while one was open for 0% of the time, Pallas kernels for 37%

profile of v1, /device:TPU:1, one launch (start us, length us, event | category | flops | bytes accessed | tf_op | source)
XLA Modules:
  0.0 142.3 jit_solution(4122787060554025804)
XLA Ops:
  0.7 5.2 %fold.1 = (f32[520,512]{1,0:T(8,128)}, f32[3,512,128]{2,1,0:T(8,128)}) custom-call(f32[1,512,1024]{2,1,0:T(8,128)} %density.1, f32[1,512]{1,0:T(1,128)} %area.1, f32[3,1,512]{2,1,0:T(1,128)} %bitcast.1, s32[2]{0:T(128)} %refs_0_.5, s32[1]{0:T(128)S(6)} %copy.13.count.refs_1_, bf16[512,1024]{1,0:T(8,128)(2,1)} %constant.4.clone.high, ...), custom_call_target="tpu_custom_call" | custom-call | tf_op jit(solution)/shard_map/fold/pallas_call | solution.py:360
  5.9 5.1 %collective-permute-start.3 = (f32[520,512]{1,0:T(8,128)}, f32[520,512]{1,0:T(8,128)}, u32[]{:S(2)}, u32[]{:S(2)}) collective-permute-start(f32[520,512]{1,0:T(8,128)} %get-tuple-element.8.refs_3_), channel_id=1, source_target_pairs={{0,14},{1,15},{2,0},{3,1},{4,2},{5,3},{6,4},{7,5},{8,6},{9,7},{10,... | collective-permute-start | bytes 3194888 | tf_op jit(solution)/shard_map/ppermute | solution.py:374
  10.9 0.0 collective-permute-start
  10.9 1.0 collective-permute-start.5
  11.9 42.4 %collective-permute-done.3.refs_3_ = f32[520,512]{1,0:T(8,128)} collective-permute-done((f32[520,512]{1,0:T(8,128)}, f32[520,512]{1,0:T(8,128)}, u32[]{:S(2)}, u32[]{:S(2)}) %collective-permute-start.3) | collective-permute-done | bytes 1064992 | tf_op jit(solution)/shard_map/ppermute | solution.py:374
  54.3 1.3 collective-permute-start.4
  55.5 1.4 %collective-permute-start.2 = (f32[520,512]{1,0:T(8,128)}, f32[520,512]{1,0:T(8,128)}, u32[]{:S(2)}, u32[]{:S(2)}) collective-permute-start(f32[520,512]{1,0:T(8,128)} %get-tuple-element.8.refs_3_), channel_id=1, source_target_pairs={{0,13},{1,4},{2,15},{3,6},{4,1},{5,8},{6,3},{7,10},{8,5},{9,12},{1... | collective-permute-start | bytes 3194888 | tf_op jit(solution)/shard_map/ppermute | solution.py:374
  56.9 0.0 collective-permute-done.refs_3_
  56.9 2.5 %collective-permute-start.1 = (f32[520,512]{1,0:T(8,128)}, f32[520,512]{1,0:T(8,128)}, u32[]{:S(2)}, u32[]{:S(2)}) collective-permute-start(f32[520,512]{1,0:T(8,128)} %collective-permute-done.refs_3_), channel_id=1, source_target_pairs={{0,1},{1,0},{2,3},{3,2},{4,5},{5,4},{6,7},{7,6},{8,9},{9,8},{10,11... | collective-permute-start | bytes 3194888 | tf_op jit(solution)/shard_map/ppermute | solution.py:374
  59.5 0.0 collective-permute-done.5.refs_4_
  59.5 26.4 %near.3.refs_5_ = f32[4,128,512]{2,1,0:T(8,128)} custom-call(s32[2]{0:T(128)} %refs_0_.5, s32[1]{0:T(128)S(6)} %copy.13.count.refs_1_, f32[3,512,128]{2,1,0:T(8,128)} %get-tuple-element.7.refs_2_, f32[520,512]{1,0:T(8,128)} %get-tuple-element.8.refs_3_, f32[520,512]{1,0:T(8,128)} %collective-permute-done.5.refs_4_), custom_call_target="tpu_custom_call" | custom-call | flops 8589934592 | bytes 4194304 | tf_op jit(solution)/shard_map/near/pallas_call | solution.py:302
  85.9 0.0 collective-permute-done.4.refs_4_
  85.9 26.6 %near.4.refs_6_ = f32[4,128,512]{2,1,0:T(8,128)} custom-call(s32[2]{0:T(128)} %refs_0_.5, s32[1]{0:T(128)S(6)} %copy.13.count.refs_1_, f32[3,512,128]{2,1,0:T(8,128)} %get-tuple-element.7.refs_2_, f32[520,512]{1,0:T(8,128)} %collective-permute-done.3.refs_3_, f32[520,512]{1,0:T(8,128)} %collective-permute-done.4.refs_4_, ...), custom_call_target="tpu_custom_call", output_to_operand_aliasing={{}: (5, {})} | custom-call | flops 8589934592 | bytes 4194304 | tf_op jit(solution)/shard_map/near/pallas_call | solution.py:302
  112.6 0.0 collective-permute-done.2.refs_5_
  112.6 0.0 collective-permute-done.1.refs_4_
  112.6 26.8 %near.5.acc = f32[4,128,512]{2,1,0:T(8,128)} custom-call(s32[2]{0:T(128)} %refs_0_.5, s32[1]{0:T(128)S(6)} %copy.13.count.refs_1_, f32[3,512,128]{2,1,0:T(8,128)} %get-tuple-element.7.refs_2_, f32[520,512]{1,0:T(8,128)} %collective-permute-done.refs_3_, f32[520,512]{1,0:T(8,128)} %collective-permute-done.1.refs_4_, ...), custom_call_target="tpu_custom_call", output_to_operand_aliasing={{}: (6, {})} | custom-call | flops 12884901888 | bytes 4194304 | tf_op jit(solution)/shard_map/near/pallas_call | solution.py:302
  139.4 2.9 %final.1 = f32[1,512,512]{2,1,0:T(8,128)} custom-call(f32[4,128,512]{2,1,0:T(8,128)} %near.5.acc, f32[1,512,512]{2,1,0:T(8,128)} %incident.1), custom_call_target="tpu_custom_call" | custom-call | tf_op jit(solution)/shard_map/final/pallas_call | solution.py:388
Async XLA Ops:
  5.9 48.4 %collective-permute-start.3 = (f32[520,512]{1,0:T(8,128)}, f32[520,512]{1,0:T(8,128)}, u32[]{:S(2)}, u32[]{:S(2)}) collective-permute-start(f32[520,512]{1,0:T(8,128)} %get-tuple-element.8.refs_3_), channel_id=1, source_target_pairs={{0,14},{1,15},{2,0},{3,1},{4,2},{5,3},{6,4},{7,5},{8,6},{9,7},{10,... | collective-permute-start | bytes 3194888 | tf_op jit(solution)/shard_map/ppermute | solution.py:374
  10.9 46.0 %collective-permute-start = (f32[520,512]{1,0:T(8,128)}, f32[520,512]{1,0:T(8,128)}, u32[]{:S(2)}, u32[]{:S(2)}) collective-permute-start(f32[520,512]{1,0:T(8,128)} %get-tuple-element.8.refs_3_), channel_id=1, source_target_pairs={{0,2},{1,3},{2,4},{3,5},{4,6},{5,7},{6,8},{7,9},{8,10},{9,11},{10,... | collective-permute-start | bytes 3194888 | tf_op jit(solution)/shard_map/ppermute | solution.py:374
  10.9 48.5 %collective-permute-start.5 = (f32[520,512]{1,0:T(8,128)}, f32[520,512]{1,0:T(8,128)}, u32[]{:S(2)}, u32[]{:S(2)}) collective-permute-start(f32[520,512]{1,0:T(8,128)} %get-tuple-element.8.refs_3_), channel_id=1, source_target_pairs={{0,1},{1,0},{2,3},{3,2},{4,5},{5,4},{6,7},{7,6},{8,9},{9,8},{10,11... | collective-permute-start | bytes 3194888 | tf_op jit(solution)/shard_map/ppermute | solution.py:374
  54.3 31.7 %collective-permute-start.4 = (f32[520,512]{1,0:T(8,128)}, f32[520,512]{1,0:T(8,128)}, u32[]{:S(2)}, u32[]{:S(2)}) collective-permute-start(f32[520,512]{1,0:T(8,128)} %collective-permute-done.3.refs_3_), channel_id=1, source_target_pairs={{0,1},{1,0},{2,3},{3,2},{4,5},{5,4},{6,7},{7,6},{8,9},{9,8},{10,11... | collective-permute-start | bytes 3194888 | tf_op jit(solution)/shard_map/ppermute | solution.py:374
  55.5 57.1 %collective-permute-start.2 = (f32[520,512]{1,0:T(8,128)}, f32[520,512]{1,0:T(8,128)}, u32[]{:S(2)}, u32[]{:S(2)}) collective-permute-start(f32[520,512]{1,0:T(8,128)} %get-tuple-element.8.refs_3_), channel_id=1, source_target_pairs={{0,13},{1,4},{2,15},{3,6},{4,1},{5,8},{6,3},{7,10},{8,5},{9,12},{1... | collective-permute-start | bytes 3194888 | tf_op jit(solution)/shard_map/ppermute | solution.py:374
  56.9 55.6 %collective-permute-start.1 = (f32[520,512]{1,0:T(8,128)}, f32[520,512]{1,0:T(8,128)}, u32[]{:S(2)}, u32[]{:S(2)}) collective-permute-start(f32[520,512]{1,0:T(8,128)} %collective-permute-done.refs_3_), channel_id=1, source_target_pairs={{0,1},{1,0},{2,3},{3,2},{4,5},{5,4},{6,7},{7,6},{8,9},{9,8},{10,11... | collective-permute-start | bytes 3194888 | tf_op jit(solution)/shard_map/ppermute | solution.py:374

commit v2 on v1

v2 whole, which is shorter than its diff:
```python
import math

import jax
import jax.numpy as jnp
import numpy as np
from jax import lax
from jax.experimental import pallas as pl
from jax.experimental.pallas import tpu as pltpu
from jax.sharding import PartitionSpec as P

COLS = 32
RADIUS = 0.95
SMOOTH = 0.01
TERMS = 23
SPAN = 4 * COLS
TILE_I = 256
TILE_J = 256
LANES = 128
KPART = 4
FAR = 7
FOLD = 256
FLAG_ROW = 3
META = 8
F32 = jnp.float32
BF16 = jnp.bfloat16
VMEM_LIMIT = 60 * 1024 * 1024
NEAR_LIMIT = 67043328


def residue_map():
    eye = np.eye(16)
    plus, minus = eye[:8] + eye[8:], eye[:8] - eye[8:]
    rows = [plus[m] + plus[m + 4] for m in range(4)]
    rows += [plus[m] - plus[m + 4] for m in range(4)]
    w = np.exp(0.25j * np.pi)
    e = minus[:4] + 1j * minus[4:]
    for sign in (1.0, -1.0):
        pair = [e[m] + sign * w * e[m + 2] for m in range(2)]
        rows += [pair[0].real, pair[1].real, pair[0].imag, pair[1].imag]
    return np.stack(rows)


def fold_table():
    steps = np.arange(16)
    angles = 2.0 * np.pi * (np.outer(steps, steps) % 16) / 16
    fold = np.stack([np.cos(angles), -np.sin(angles)], axis=2).reshape(16, 32) / 16
    return residue_map() @ fold


def nodes_of(group):
    offset = (0, 2, 1, 3)[group]
    table = np.abs(fold_table()[group * 4 : group * 4 + 4]).reshape(4, 16, 2).max(axis=(0, 2))
    nodes = [l for l in range(16) if table[l] > 1e-9]
    assert len(nodes) == 4 and offset in nodes
    return nodes


def scales():
    inv = [1.0] * (TERMS + 1)
    for n in range(3, TERMS):
        inv[n + 1] = inv[n] * 2.0 * RADIUS / (n + 1)
    return inv


def split(value):
    high = value.astype(BF16)
    return high, (value - high.astype(F32)).astype(BF16)


def dot_nt(left, right):
    return lax.dot_general(left, right, (((1,), (1,)), ((), ())), preferred_element_type=F32)


def live_ahead(listed, count, delta):
    devices = lax.axis_size("clus")
    wanted = lax.rem(lax.axis_index("clus") + delta + devices, devices)
    first = (listed[0] == wanted) & (count[0] > 0)
    second = (listed[1] == wanted) & (count[0] > 1)
    return first | second


def fold_kernel(density, area, place, listed, count, out, turned):
    turned[...] = density[0].T
    table = fold_table()
    for group in range(4):
        nodes = nodes_of(group)
        for n in range(4):
            index = group * 4 + n
            total = None
            for entry in [2 * l + part for l in nodes for part in range(2)]:
                term = float(table[index, entry]) * turned[entry * COLS : (entry + 1) * COLS, :]
                total = term if total is None else total + term
            out[index * COLS : (index + 1) * COLS, :] = total * area[...]
    rows = 16 * COLS
    width = out.shape[1]
    for axis in range(3):
        out[rows + axis : rows + axis + 1, :] = place[axis]
    for ahead in range(1, 4):
        flag = jnp.where(live_ahead(listed, count, ahead), 1.0, 0.0).astype(F32)
        row = rows + FLAG_ROW + ahead - 1
        out[row : row + 1, :] = jnp.full((1, width), flag, F32)
    out[rows + 6 : rows + 8, :] = jnp.zeros((2, width), F32)


def kernels(targets, sources):
    inv = scales()
    gaps = [a - b for a, b in zip(targets, sources)]
    square = gaps[0] * gaps[0] + gaps[1] * gaps[1] + gaps[2] * gaps[2] + SMOOTH
    inverse = lax.rsqrt(square)
    dist = square * inverse
    t = [jnp.exp(-1.5 * dist) * inverse]
    t.append((2.0 * RADIUS) * dist * t[0])
    for n in range(1, 3):
        t.append(dist * ((2.0 * RADIUS / (n + 1)) * t[n] - (RADIUS * RADIUS / (n + 1)) * t[n - 1]))
    for n in range(3, TERMS):
        factor = RADIUS * inv[n - 1] / (2.0 * inv[n])
        t.append(dist * (t[n] - factor * t[n - 1]))
    plus, minus = [], []
    for m in range(8):
        base = t[m]
        if m + 16 <= TERMS:
            base = base + (inv[m + 16] / inv[m]) * t[m + 16]
        other = (inv[m + 8] / inv[m]) * t[m + 8]
        plus.append(base + other)
        minus.append(base - other)
    first, second = [], []
    for m in range(4):
        other = inv[m + 4] * plus[m + 4]
        first.append(plus[m] + other)
        second.append(plus[m] - other)
    third, fourth = [], []
    half = math.sqrt(0.5)
    for m in range(2):
        a = half * minus[m + 2]
        b = (half * inv[m + 6]) * minus[m + 6]
        imag = inv[m + 4] * minus[m + 4]
        third += [minus[m] + (a - b), imag + (a + b)]
        fourth += [minus[m] - (a - b), imag - (a + b)]
    return first + second + third + fourth


def prepare(slot, payload, lhs, spots):
    panels = payload.shape[1]
    half = math.sqrt(0.5)
    rows = 16 * COLS

    def column(j, carry):
        at = pl.ds(pl.multiple_of(j * LANES, LANES), LANES)
        spots[slot, j] = payload[rows : rows + META, at]

        def block(index, part):
            top = index * COLS + part * 16
            return payload[top : top + 16, at]

        def put(kernel, position, part, pieces):
            top = position * COLS + part * 16
            lhs[slot, kernel, j, top : top + 16, :] = pieces[0]
            lhs[slot, kernel, j, SPAN + top : SPAN + top + 16, :] = pieces[1]

        for group in range(4):
            for part in range(COLS // 16):
                raw = [block(group * 4 + n, part) for n in range(4)]
                if group < 2:
                    pieces = [split(r) for r in raw]
                    flipped = [split(-r) for r in raw] if group else pieces
                    table = [
                        [pieces[n - k] if n >= k else flipped[n - k + 4] for n in range(4)]
                        for k in range(4)
                    ]
                else:
                    sign = half if group == 2 else -half
                    x0r, x1r, x0i, x1i = [split(r) for r in raw]
                    n0i, n1i = split(-raw[2]), split(-raw[3])
                    turned = sign * (raw[1] + raw[3])
                    wr, wi, nwi = split(sign * (raw[1] - raw[3])), split(turned), split(-turned)
                    table = [
                        [x0r, x1r, x0i, x1i],
                        [n0i, n1i, x0r, x1r],
                        [wr, x0r, wi, x0i],
                        [nwi, n0i, wr, x0r],
                    ]
                for k in range(4):
                    for n in range(4):
                        put(group * 4 + k, n, part, table[k][n])
        return carry

    lax.fori_loop(0, panels // LANES, column, 0)


def near_kernel(sources, has_input, last, *refs):
    count = len(sources)
    regions = 3 if last else 2
    metas_hbm = refs[0:2]
    payload_hbm = refs[2 : 2 + count]
    rest = refs[2 + count :]
    before_hbm = rest[0] if has_input else None
    outs = rest[1:] if has_input else rest
    payloads, metas, own, acc, lhs, spots, high0, low0, high1, low1, items, sems = outs[-12:]
    outs = outs[:-12]
    core = lax.rem(lax.axis_index("clus"), 2)
    rows = 16 * COLS
    head = acc.at[:, 0:SPAN, 0 : 2 * TILE_I]
    loads = [
        pltpu.make_async_copy(payload_hbm[s], payloads.at[s], sems.at[4 + s]) for s in range(count)
    ]
    info = [
        pltpu.make_async_copy(
            metas_hbm[m].at[pl.ds(rows, META), :], metas.at[core if m == 0 else 1 - core], sems.at[2 + m]
        )
        for m in range(2)
    ]
    for load in info + loads:
        load.start()
    for load in info + loads:
        load.wait()

    def flag(meta, distance):
        row = FLAG_ROW - 1 + jnp.clip(distance, 1, 3)
        return (jnp.max(meta(row)) > 0.5) & (distance >= 1) & (distance <= 3)

    total = jnp.int32(0)
    used = []
    for s, (base, slope) in enumerate(sources):
        lives = []
        for t in range(2):
            delta = base + slope * core - t
            ahead = flag(lambda row: metas[t, pl.ds(row, 1), :], delta)
            behind = flag(lambda row: payloads[s, pl.ds(rows + row, 1), :], -delta)
            lives.append((delta == 0) | ahead | behind)
        used.append(lives[0] | lives[1])
        if slope == FAR:
            lives.append(used[-1])
        for region, live in enumerate(lives):

            @pl.when(live)
            def _():
                items[0, total] = s
                items[1, total] = region

            total = total + live.astype(jnp.int32)

    def body():
        if has_input:
            before_load = pltpu.make_async_copy(before_hbm, head, sems.at[0])
            before_load.start()
        else:
            head[...] = jnp.zeros(head.shape, F32)
        if last:
            acc[:, 0:SPAN, 2 * TILE_I :] = jnp.zeros((4, SPAN, TILE_I), F32)
        acc[:, SPAN : 2 * SPAN, :] = jnp.zeros((4, SPAN, regions * TILE_I), F32)
        high1[...] = jnp.zeros_like(high1)
        low1[...] = jnp.zeros_like(low1)
        for region in range(regions):
            cluster = core if region == 2 else region
            side = 1 - core if region == 2 else core
            at = pl.ds(pl.multiple_of(side * TILE_I, TILE_I), TILE_I)
            for axis in range(3):
                line = metas[cluster, axis : axis + 1, at]
                own[axis, region * TILE_I : (region + 1) * TILE_I, :] = jnp.broadcast_to(line, (LANES, TILE_I)).T
        for s in range(count):

            @pl.when(used[s])
            def _():
                prepare(s, payloads.at[s], lhs, spots)

        if has_input:
            before_load.wait()
        near_body(total, own, acc, lhs, spots, high0, low0, high1, low1, items)
        acc[:, 0:SPAN, :] = acc[:, 0:SPAN, :] + acc[:, SPAN : 2 * SPAN, :]

    if last:
        body()

        def region_of(index):
            return acc.at[:, 0:SPAN, pl.ds(pl.multiple_of(index * TILE_I, TILE_I), TILE_I)]

        keep, send = outs
        stores = [
            pltpu.make_async_copy(region_of(core), keep.at[:, :, 0:TILE_I], sems.at[0]),
            pltpu.make_async_copy(region_of(2), keep.at[:, :, TILE_I : 2 * TILE_I], sems.at[1]),
            pltpu.make_async_copy(region_of(1 - core), send, sems.at[2]),
        ]
        for store in stores:
            store.start()
        for store in stores:
            store.wait()
    else:

        @pl.when(total > 0)
        def _():
            body()
            store = pltpu.make_async_copy(head, outs[0], sems.at[1])
            store.start()
            store.wait()


def near_body(total, own, acc, lhs, spots, high0, low0, high1, low1, items):
    halves = TILE_J // LANES

    def evaluate(slot, j, region, high, low, quarter):
        for r in range(KPART):
            row = pl.multiple_of((quarter * KPART + r) * 16, 16)
            at = pl.multiple_of(region * TILE_I + row, 16)
            targets = [own[a, pl.ds(at, 16), :] for a in range(3)]
            for h in range(halves):
                spot = spots[slot, j * halves + h]
                sources = [jnp.broadcast_to(spot[a : a + 1, :], (16, LANES)) for a in range(3)]
                for index, value in enumerate(kernels(targets, sources)):
                    top, bottom = split(value)
                    high[index, h, pl.ds(row, 16), :] = top
                    low[index, h, pl.ds(row, 16), :] = bottom

    def joined(read):
        return jnp.concatenate([read(k, h) for k in range(KPART) for h in range(halves)], axis=1)

    def apply(slot, j, region, high, low, part):
        first = part * KPART
        group = first // 4
        left = joined(lambda k, h: lhs[slot, first + k, j * halves + h])
        at = pl.ds(pl.multiple_of(region * TILE_I, TILE_I), TILE_I)
        acc[group, :, at] += dot_nt(left, joined(lambda k, h: high[first + k, h]))
        acc[group, 0:SPAN, at] += dot_nt(left[0:SPAN], joined(lambda k, h: low[first + k, h]))

    def step(index, carry):
        slot, region = items[0, index], items[1, index]
        before = jnp.maximum(index - 1, 0)
        slot_before, region_before = items[0, before], items[1, before]

        def first(part, c):
            evaluate(slot, 0, region, high0, low0, part)
            apply(slot_before, 1, region_before, high1, low1, part)
            return c

        def second(part, c):
            evaluate(slot, 1, region, high1, low1, part)
            apply(slot, 0, region, high0, low0, part)
            return c

        lax.fori_loop(0, 16 // KPART, first, 0)
        lax.fori_loop(0, 16 // KPART, second, 0)
        return carry

    lax.fori_loop(0, total, step, 0)

    @pl.when(total > 0)
    def _():
        slot, region = items[0, total - 1], items[1, total - 1]

        def rest(part, c):
            apply(slot, 1, region, high1, low1, part)
            return c

        lax.fori_loop(0, 16 // KPART, rest, 0)


def near_call(metas, sources, payloads, acc, last=False):
    count = len(payloads)
    panels = payloads[0].shape[1]
    tiles = panels // LANES
    regions = 3 if last else 2
    shape = jax.ShapeDtypeStruct((4, SPAN, 2 * TILE_I), F32)
    anywhere = pl.BlockSpec(memory_space=pl.ANY)
    arguments = [*metas, *payloads] + ([] if acc is None else [acc])
    return pl.pallas_call(
        lambda *refs: near_kernel(sources, acc is not None, last, *refs),
        out_shape=(shape, jax.ShapeDtypeStruct((4, SPAN, TILE_I), F32)) if last else shape,
        in_specs=[anywhere] * len(arguments),
        out_specs=(anywhere, anywhere) if last else anywhere,
        input_output_aliases={} if acc is None or last else {len(arguments) - 1: 0},
        scratch_shapes=[
            pltpu.VMEM((count,) + payloads[0].shape, F32),
            pltpu.VMEM((2, META, panels), F32),
            pltpu.VMEM((3, regions * TILE_I, LANES), F32),
            pltpu.VMEM((4, 2 * SPAN, regions * TILE_I), F32),
            pltpu.VMEM((count, 16, tiles, 2 * SPAN, LANES), BF16),
            pltpu.VMEM((count, tiles, META, LANES), F32),
        ]
        + [pltpu.VMEM((16, TILE_J // LANES, TILE_I, LANES), BF16)] * 4
        + [pltpu.SMEM((2, 16), jnp.int32), pltpu.SemaphoreType.DMA((4 + count,))],
        compiler_params=pltpu.CompilerParams(vmem_limit_bytes=NEAR_LIMIT),
        cost_estimate=pl.CostEstimate(
            flops=count * 2 * 32768 * 256 * 256, bytes_accessed=4 << 20, transcendentals=0
        ),
        name="near",
    )(*arguments)


def final_kernel(keep, received, incident, out):
    core = lax.rem(lax.axis_index("clus"), 2)
    half = math.sqrt(0.5)
    for local in range(0, 2 * TILE_I, LANES):
        near_half = local < TILE_I
        side = core if near_half else 1 - core
        row = pl.multiple_of(side * TILE_I + local % TILE_I, LANES)
        at = pl.ds(row, LANES)
        parts = []
        for group in range(4):
            whole = keep[group, :, local : local + LANES]
            if not near_half:
                whole = whole + received[group, :, local - TILE_I : local - TILE_I + LANES]
            parts.append([whole[n * COLS : (n + 1) * COLS] for n in range(4)])
        first, second, third, fourth = parts
        plus = [first[n] + second[n] for n in range(4)] + [first[n] - second[n] for n in range(4)]
        minus = [None] * 8
        for m in range(2):
            sum_r, sum_i = third[m] + fourth[m], third[m + 2] + fourth[m + 2]
            gap_r, gap_i = third[m] - fourth[m], third[m + 2] - fourth[m + 2]
            minus[m], minus[m + 4] = sum_r, sum_i
            minus[m + 2] = half * (gap_r + gap_i)
            minus[m + 6] = half * (gap_i - gap_r)
        steps = [None] * 16
        for m in range(8):
            low = plus[m] + minus[m]
            high = plus[m] - minus[m]
            for n, value in ((-m % 16, low), ((-m - 8) % 16, high)):
                steps[n] = value * (0.25 * RADIUS ** (-n))
        potential = jnp.concatenate(steps, axis=0).T
        out[0, at, :] = incident[0, at, :] - potential


def residual(density, positions, area, incident, pair_list, pair_count):
    devices = lax.axis_size("clus")
    panels = positions.shape[2]
    pairs = (pair_list, pair_count)
    vmem = pl.BlockSpec(memory_space=pltpu.VMEM)
    smem = pl.BlockSpec(memory_space=pltpu.SMEM)
    payload = pl.pallas_call(
        fold_kernel,
        out_shape=jax.ShapeDtypeStruct((16 * COLS + META, panels), F32),
        grid=(panels // FOLD,),
        in_specs=[
            pl.BlockSpec((1, FOLD, density.shape[2]), lambda p: (0, p, 0)),
            pl.BlockSpec((1, FOLD), lambda p: (0, p)),
            pl.BlockSpec((3, 1, FOLD), lambda p: (0, 0, p)),
            smem,
            smem,
        ],
        out_specs=pl.BlockSpec((16 * COLS + META, FOLD), lambda p: (0, p)),
        scratch_shapes=[pltpu.VMEM((density.shape[2], FOLD), F32)],
        compiler_params=pltpu.CompilerParams(vmem_limit_bytes=VMEM_LIMIT),
        name="fold",
    )(density, area, positions.transpose(1, 0, 2), *pairs)

    def route(value, move, members=lambda k: True):
        pairs_of = [(k, move(k) % devices) for k in range(devices) if members(k)]
        return lax.ppermute(value, "clus", pairs_of)

    def swap(value):
        return route(value, lambda k: k ^ 1)

    partner = swap(payload)
    ahead = route(payload, lambda k: k - 2)
    far = route(payload, lambda k: k - 3 if k % 2 == 0 else k + 3)
    behind = route(payload, lambda k: k + 2)
    metas = (payload, partner)
    acc = near_call(metas, ((0, 1), (1, -1)), (payload, partner), None)
    ahead_other = swap(ahead)
    acc = near_call(metas, ((2, 1), (3, -1)), (ahead, ahead_other), acc)
    behind_other = swap(behind)
    keep, send = near_call(
        metas, ((-2, 1), (-1, -1), (-3, FAR)), (behind, behind_other, far), acc, True
    )
    received = swap(send)
    return pl.pallas_call(
        final_kernel,
        out_shape=jax.ShapeDtypeStruct(incident.shape, F32),
        in_specs=[vmem] * 3,
        out_specs=vmem,
        compiler_params=pltpu.CompilerParams(vmem_limit_bytes=VMEM_LIMIT),
        name="final",
    )(keep, received, incident)


def solution(mesh):
    spec3 = P(("parts", "clus"), None, None)
    in_specs = (spec3, spec3, P(("parts", "clus"), None), spec3, P(("parts", "clus")), P(("parts", "clus")))
    return jax.shard_map(residual, mesh=mesh, in_specs=in_specs, out_specs=spec3, check_vma=False)
```

time: 143 us -> 138 us (0.965)
  the two profiles are of different devices: /device:TPU:1 before, /device:TPU:0 now
where the time goes in v2:
time: 138 us
  Pallas kernels  80.4 us (58%)
  waiting for transfers between devices  45.7 us (33%)
  starting transfers between devices  10.1 us (7%)
    pallas_call x3, Pallas kernels, near_call(): pl.pallas_call(lambda *refs: near_kernel(sources, acc is not None, last,...  74.4 us
    ppermute x7, waiting for transfers between devices, route(): return lax.ppermute(value, 'clus', pairs_of)  45.7 us
    ppermute x7, starting transfers between devices, route(): return lax.ppermute(value, 'clus', pairs_of)  10.1 us
    pallas_call x1, Pallas kernels, residual(): pl.pallas_call(final_kernel, out_shape=jax.ShapeDtypeStruct(incident.shap...  3.06 us
    pallas_call x1, Pallas kernels, residual(): pl.pallas_call(fold_kernel, out_shape=jax.ShapeDtypeStruct((16 * COLS + M...  2.89 us
  transfers between devices with their start and end apart: 7, of which 2 were waited for; matrix products, arithmetic and copies ran while one was open for 0% of the time, Pallas kernels for 31%

profile of v2, /device:TPU:0, one launch (start us, length us, event | category | flops | bytes accessed | tf_op | source)
XLA Modules:
  0.0 137.7 jit_solution(9104093811856122605)
XLA Ops:
  0.7 2.9 %fold.1.refs_0_.refs_2_ = f32[520,512]{1,0:T(8,128)} custom-call(f32[1,512,1024]{2,1,0:T(8,128)} %density.1, f32[1,512]{1,0:T(1,128)} %area.1, f32[3,1,512]{2,1,0:T(1,128)} %bitcast.1, s32[2]{0:T(128)} %listed.1, s32[1]{0:T(128)S(6)} %copy.9.count), custom_call_target="tpu_custom_call" | custom-call | tf_op jit(solution)/shard_map/fold/pallas_call | solution.py:427
  3.5 6.0 %collective-permute-start.4 = (f32[520,512]{1,0:T(8,128)}, f32[520,512]{1,0:T(8,128)}, u32[]{:S(2)}, u32[]{:S(2)}) collective-permute-start(f32[520,512]{1,0:T(8,128)} %fold.1.refs_0_.refs_2_), channel_id=1, source_target_pairs={{0,14},{1,15},{2,0},{3,1},{4,2},{5,3},{6,4},{7,5},{8,6},{9,7},{10,... | collective-permute-start | bytes 3194888 | tf_op jit(solution)/shard_map/ppermute | solution.py:446
  9.5 0.0 collective-permute-start.1
  9.5 0.0 collective-permute-start
  9.5 43.6 %collective-permute-done.4.refs_2_ = f32[520,512]{1,0:T(8,128)} collective-permute-done((f32[520,512]{1,0:T(8,128)}, f32[520,512]{1,0:T(8,128)}, u32[]{:S(2)}, u32[]{:S(2)}) %collective-permute-start.4) | collective-permute-done | bytes 1064992 | tf_op jit(solution)/shard_map/ppermute | solution.py:446
  53.1 0.0 collective-permute-start.5
  53.2 4.0 %collective-permute-start.3 = (f32[520,512]{1,0:T(8,128)}, f32[520,512]{1,0:T(8,128)}, u32[]{:S(2)}, u32[]{:S(2)}) collective-permute-start(f32[520,512]{1,0:T(8,128)} %fold.1.refs_0_.refs_2_), channel_id=1, source_target_pairs={{0,13},{1,4},{2,15},{3,6},{4,1},{5,8},{6,3},{7,10},{8,5},{9,12},{1... | collective-permute-start | bytes 3194888 | tf_op jit(solution)/shard_map/ppermute | solution.py:446
  57.1 0.0 collective-permute-done.1.refs_2_
  57.1 0.0 collective-permute-start.2
  57.1 0.0 collective-permute-done.refs_1_.refs_3_
  57.1 26.2 %near.3.refs_4_ = f32[4,128,512]{2,1,0:T(8,128)} custom-call(f32[520,512]{1,0:T(8,128)} %fold.1.refs_0_.refs_2_, f32[520,512]{1,0:T(8,128)} %collective-permute-done.refs_1_.refs_3_, f32[520,512]{1,0:T(8,128)} %fold.1.refs_0_.refs_2_, f32[520,512]{1,0:T(8,128)} %collective-permute-done.refs_1_.refs_3_), custom_call_target="tpu_custom_call" | custom-call | flops 8589934592 | bytes 4194304 | tf_op jit(solution)/shard_map/near/pallas_call | solution.py:364
  83.3 0.0 collective-permute-done.5.refs_3_
  83.4 16.2 %near.4.refs_5_ = f32[4,128,512]{2,1,0:T(8,128)} custom-call(f32[520,512]{1,0:T(8,128)} %fold.1.refs_0_.refs_2_, f32[520,512]{1,0:T(8,128)} %collective-permute-done.refs_1_.refs_3_, f32[520,512]{1,0:T(8,128)} %collective-permute-done.4.refs_2_, f32[520,512]{1,0:T(8,128)} %collective-permute-done.5.refs_3_, ...), custom_call_target="tpu_custom_call", output_to_operand_aliasing={{}: (4, {})} | custom-call | flops 8589934592 | bytes 4194304 | tf_op jit(solution)/shard_map/near/pallas_call | solution.py:364
  99.6 0.0 collective-permute-done.3.refs_4_
  99.6 0.0 collective-permute-done.2.refs_3_
  99.6 32.0 %near.5 = (f32[4,128,512]{2,1,0:T(8,128)}, f32[4,128,256]{2,1,0:T(8,128)}) custom-call(f32[520,512]{1,0:T(8,128)} %fold.1.refs_0_.refs_2_, f32[520,512]{1,0:T(8,128)} %collective-permute-done.refs_1_.refs_3_, f32[520,512]{1,0:T(8,128)} %collective-permute-done.1.refs_2_, f32[520,512]{1,0:T(8,128)} %collective-permute-done.2.refs_3_, ...), custom_call_target="tpu_custom_call" | custom-call | flops 12884901888 | bytes 4194304 | tf_op jit(solution)/shard_map/near/pallas_call | solution.py:364
  131.6 0.1 collective-permute-start.6
  131.7 2.1 %collective-permute-done.6.received = f32[4,128,256]{2,1,0:T(8,128)S(1)} collective-permute-done((f32[4,128,256]{2,1,0:T(8,128)}, f32[4,128,256]{2,1,0:T(8,128)S(1)}, u32[]{:S(2)}, u32[]{:S(2)}) %collective-permute-start.6) | collective-permute-done | bytes 524320 | tf_op jit(solution)/shard_map/ppermute | solution.py:446
  133.8 0.0 copy-start
  133.8 0.8 copy-done
  134.6 3.1 %final.1 = f32[1,512,512]{2,1,0:T(8,128)} custom-call(f32[4,128,512]{2,1,0:T(8,128)} %get-tuple-element.7.keep, f32[4,128,256]{2,1,0:T(8,128)} %copy-done, f32[1,512,512]{2,1,0:T(8,128)} %incident.1), custom_call_target="tpu_custom_call" | custom-call | tf_op jit(solution)/shard_map/final/pallas_call | solution.py:464
Async XLA Ops:
  3.5 49.6 %collective-permute-start.4 = (f32[520,512]{1,0:T(8,128)}, f32[520,512]{1,0:T(8,128)}, u32[]{:S(2)}, u32[]{:S(2)}) collective-permute-start(f32[520,512]{1,0:T(8,128)} %fold.1.refs_0_.refs_2_), channel_id=1, source_target_pairs={{0,14},{1,15},{2,0},{3,1},{4,2},{5,3},{6,4},{7,5},{8,6},{9,7},{10,... | collective-permute-start | bytes 3194888 | tf_op jit(solution)/shard_map/ppermute | solution.py:446
  9.5 47.6 %collective-permute-start.1 = (f32[520,512]{1,0:T(8,128)}, f32[520,512]{1,0:T(8,128)}, u32[]{:S(2)}, u32[]{:S(2)}) collective-permute-start(f32[520,512]{1,0:T(8,128)} %fold.1.refs_0_.refs_2_), channel_id=1, source_target_pairs={{0,2},{1,3},{2,4},{3,5},{4,6},{5,7},{6,8},{7,9},{8,10},{9,11},{10,... | collective-permute-start | bytes 3194888 | tf_op jit(solution)/shard_map/ppermute | solution.py:446
  9.5 47.6 %collective-permute-start = (f32[520,512]{1,0:T(8,128)}, f32[520,512]{1,0:T(8,128)}, u32[]{:S(2)}, u32[]{:S(2)}) collective-permute-start(f32[520,512]{1,0:T(8,128)} %fold.1.refs_0_.refs_2_), channel_id=1, source_target_pairs={{0,1},{1,0},{2,3},{3,2},{4,5},{5,4},{6,7},{7,6},{8,9},{9,8},{10,11... | collective-permute-start | bytes 3194888 | tf_op jit(solution)/shard_map/ppermute | solution.py:446
  53.1 30.2 %collective-permute-start.5 = (f32[520,512]{1,0:T(8,128)}, f32[520,512]{1,0:T(8,128)}, u32[]{:S(2)}, u32[]{:S(2)}) collective-permute-start(f32[520,512]{1,0:T(8,128)} %collective-permute-done.4.refs_2_), channel_id=1, source_target_pairs={{0,1},{1,0},{2,3},{3,2},{4,5},{5,4},{6,7},{7,6},{8,9},{9,8},{10,11... | collective-permute-start | bytes 3194888 | tf_op jit(solution)/shard_map/ppermute | solution.py:446
  53.2 46.4 %collective-permute-start.3 = (f32[520,512]{1,0:T(8,128)}, f32[520,512]{1,0:T(8,128)}, u32[]{:S(2)}, u32[]{:S(2)}) collective-permute-start(f32[520,512]{1,0:T(8,128)} %fold.1.refs_0_.refs_2_), channel_id=1, source_target_pairs={{0,13},{1,4},{2,15},{3,6},{4,1},{5,8},{6,3},{7,10},{8,5},{9,12},{1... | collective-permute-start | bytes 3194888 | tf_op jit(solution)/shard_map/ppermute | solution.py:446
  57.1 42.5 %collective-permute-start.2 = (f32[520,512]{1,0:T(8,128)}, f32[520,512]{1,0:T(8,128)}, u32[]{:S(2)}, u32[]{:S(2)}) collective-permute-start(f32[520,512]{1,0:T(8,128)} %collective-permute-done.1.refs_2_), channel_id=1, source_target_pairs={{0,1},{1,0},{2,3},{3,2},{4,5},{5,4},{6,7},{7,6},{8,9},{9,8},{10,11... | collective-permute-start | bytes 3194888 | tf_op jit(solution)/shard_map/ppermute | solution.py:446
  131.6 2.2 %collective-permute-start.6 = (f32[4,128,256]{2,1,0:T(8,128)}, f32[4,128,256]{2,1,0:T(8,128)S(1)}, u32[]{:S(2)}, u32[]{:S(2)}) collective-permute-start(f32[4,128,256]{2,1,0:T(8,128)} %get-tuple-element.8), channel_id=1, source_target_pairs={{0,1},{1,0},{2,3},{3,2},{4,5},{5,4},{6,7},{7,6},{8,9},{9,8},{10,11... | collective-permute-start | bytes 1572872 | tf_op jit(solution)/shard_map/ppermute | solution.py:446
  133.8 0.8 copy-start
